TPU v7x, 32 devices: a whole 2x2x4 slice. The times are simulated.
32 devices in a mesh: grp: 4 (over z), sep: 8 (over y, x, core).
Axes of the slice: x: 2, y: 2, z: 4, core: 2. Of those that a mesh axis runs over, the one named last changes fastest.
Arguments:
- tiles: bfloat16 [4, 256, 64, 128], P('grp', 'sep'), may hold values from 0.0099487305 to 0.29882812
- tile_front: int32 [4, 256, 1], P('grp', 'sep'), may hold values from 0 to 7; in each aligned block of 32 rows (0 to 31, 32 to 63, ..., all dimensions but the last counted through in order) at most 8 rows name the same one
- tile_pos: int32 [4, 256], P('grp', 'sep'), may hold values from 0 to 29
- front_slot: int32 [4, 8], P('grp'), may hold values from 0 to 7, as said below
- front_parent: int32 [4, 8], P('grp'), may hold values from 0 to 7, as said below
- pivot: float32 [4, 8, 640], P('grp'), may hold values from 4 to 40
Outputs:
- factor: float32 [4, 8, 640, 512], P('grp', 'sep')
- sep_schur: float32 [8, 128, 128], P('sep')
Inputs may be any that keep to these rules, and one draw needn't show every extreme that they name: `tile_front`: at most 8 of the tiles held by one device belong to one front. `front_slot`: each group's row is a permutation of 0 to 7. (front_parent[g, f] - front_slot[g, f]) modulo 8 is one of 0, 1, 7 and 4; in every group each of these four occurs.
All inputs are finite; a program needn't handle non-finite values.
Results may differ from a plain program's by a relative error of at most 0.0003.
Values may be sent and summed in bfloat16 or wider, within the bound.
A program may use at most 64 MiB of HBM per device.

v0:
```python
import jax
import jax.numpy as jnp
import numpy as np
from jax import lax
from jax.sharding import PartitionSpec as P

POS = 30


def passed_along(shard, axis, by):
    devices = lax.axis_size(axis)
    return lax.ppermute(shard, axis, [(i, (i + by) % devices) for i in range(devices)])


def tile_arrangement(rows, column_indices):
    row_count = 5 * column_indices // rows
    position = np.zeros((row_count, 5), np.int32)
    present = np.zeros((row_count, 5), np.float32)
    number = 0
    for row_block in range(row_count):
        for col_block in range(row_block * rows // column_indices + 1):
            position[row_block, col_block] = number
            present[row_block, col_block] = 1.0
            number += 1
    return (position, present)


def front_factor(summed, pivots, rows, column_indices):
    position, present = tile_arrangement(rows, column_indices)
    order = 5 * column_indices
    elimination_count = 4 * column_indices
    blocks = summed[position] * jnp.asarray(present, jnp.float32)[:, :, None, None]
    full = blocks.transpose(0, 2, 1, 3).reshape(order, order)
    mixed = 0.5 * (full + full.T) * (1.0 - jnp.eye(order, dtype=jnp.float32))
    front_matrix = jnp.diag(pivots + jnp.sum(mixed, 1)) - mixed
    lower_triangle = jnp.linalg.cholesky(front_matrix[:elimination_count, :elimination_count])
    under_diagonal = jax.scipy.linalg.solve_triangular(
        lower_triangle, front_matrix[elimination_count:, :elimination_count].T, lower=True
    ).T
    schur = jnp.dot(under_diagonal, under_diagonal.T, precision=lax.Precision.HIGHEST)
    return (jnp.concatenate([lower_triangle, under_diagonal], 0), schur)


def body(tiles, tile_front, tile_pos, front_slot, front_parent, pivot):
    width = lax.axis_size("sep")
    myself = lax.axis_index("sep")
    held = tiles.shape[1]
    rows = tiles.shape[2]
    column_indices = tiles.shape[3]
    fronts = front_slot.shape[1]
    room = max(2, -(-2 * held // width))
    slots = front_slot[0]
    parents = front_parent[0]
    front_ids = jnp.arange(fronts, dtype=jnp.int32)
    owner_of = jnp.sum(jnp.where(tile_front[0] == front_ids[None, :], slots[None, :], 0), 1)
    target = (owner_of[:, None] == jnp.arange(width, dtype=jnp.int32)[None, :]).astype(jnp.int32)
    rank = jnp.sum(target * (jnp.cumsum(target, 0) - 1), 1)
    place = owner_of * room + rank
    outgoing = jnp.zeros((width * room, rows, column_indices), jnp.bfloat16).at[place].set(tiles[0])
    labels = jnp.full((width * room,), -1, jnp.int32).at[place].set(tile_pos[0])
    arrived, received_position = (
        lax.all_to_all(
            outgoing.reshape(width, room, rows, column_indices),
            "sep",
            split_axis=0,
            concat_axis=0,
            tiled=True,
        ),
        lax.all_to_all(labels.reshape(width, room), "sep", split_axis=0, concat_axis=0, tiled=True),
    )
    arrived = arrived.reshape(width * room, rows, column_indices)
    received_position = received_position.reshape(width * room)
    selector = (received_position[None, :] == jnp.arange(POS, dtype=jnp.int32)[:, None]).astype(
        jnp.bfloat16
    )
    summed = jnp.einsum("ps,sij->pij", selector, arrived, preferred_element_type=jnp.float32)
    mine = slots == myself
    pivots = jnp.sum(jnp.where(mine[:, None], pivot[0], 0.0), 0)
    parent = jnp.sum(jnp.where(mine, parents, 0))
    factor, schur = front_factor(summed, pivots, rows, column_indices)
    distance = (parent - myself) % width
    local_sum = jnp.where(distance == 0, schur, 0.0)[None]
    for offset in (1, -1, width // 2):
        piece = jnp.where(distance == offset % width, schur, 0.0)[None]
        local_sum = local_sum + passed_along(piece, "sep", offset)
    total = lax.psum(local_sum, "grp")
    return (factor[None, None], total)


def solution(mesh):
    placed = (
        P("grp", "sep", None, None),
        P("grp", "sep", None),
        P("grp", "sep"),
        P("grp", None),
        P("grp", None),
        P("grp", None, None),
    )
    return jax.shard_map(
        body,
        mesh=mesh,
        in_specs=placed,
        out_specs=(P("grp", "sep", None, None), P("sep", None, None)),
        check_vma=False,
    )
```

profile of v0, /device:TPU:0, one launch (start us, length us, event | category | flops | bytes accessed | tf_op | source)
XLA Modules:
  0.0 244.2 jit_solution(3018031008141978505)
XLA Ops:
  9.8 5.2 %all-to-all-start = ((s32[8,1,8]{2,1,0:T(1,128)}), s32[8,1,8]{2,1,0:T(1,128)S(1)}, u32[]{:S(2)}, u32[]{:S(2)}) async-start(s32[8,1,8]{2,1,0:T(1,128)} %bitcast.6), calls=%async_computation | async-start | bytes 8192 | tf_op jit(solution)/shard_map/all_to_all | solution.py:69
  15.3 3.4 %scatter_fusion = bf16[64,64,128]{2,1,0:T(8,128)(2,1)S(1)} fusion(bf16[64,64,128]{2,1,0:T(8,128)(2,1)S(1)} %broadcast_in_dim.90, s32[32]{0:T(128)S(1)} %fusion.44, bf16[32,64,128]{2,1,0:T(8,128)(2,1)} %bitcast.120), kind=kCustom, calls=%fused_computation.2 | custom fusion | bytes 1572992 | tf_op jit(solution)/shard_map/scatter | solution.py:59
  18.7 1.7 copy.28
  20.4 4.2 %all-to-all-start.1 = ((bf16[8,8,64,128]{3,1,2,0:T(8,128)(2,1)}), bf16[8,8,64,128]{3,1,2,0:T(8,128)(2,1)S(1)}, u32[]{:S(2)}, u32[]{:S(2)}) async-start(bf16[8,8,64,128]{3,1,2,0:T(8,128)(2,1)} %copy.28), calls=%async_computation.1 | async-start | bytes 2097152 | tf_op jit(solution)/shard_map/all_to_all | solution.py:62
  27.4 12.6 %all-to-all-done.1 = bf16[8,8,64,128]{3,1,2,0:T(8,128)(2,1)S(1)} async-done(((bf16[8,8,64,128]{3,1,2,0:T(8,128)(2,1)}), bf16[8,8,64,128]{3,1,2,0:T(8,128)(2,1)S(1)}, u32[]{:S(2)}, u32[]{:S(2)}) %all-to-all-start.1) | async-done | bytes 1048608 | tf_op jit(solution)/shard_map/all_to_all | solution.py:62
  42.7 1.6 copy.49
  44.3 2.7 %copy.32 = f32[640,640]{0,1:T(8,128)} copy(f32[640,640]{1,0:T(8,128)} %bitcast.118) | data formatting | bytes 3276800 | tf_op jit(solution)/shard_map/reshape | solution.py:33
  47.0 2.0 fusion.7
  49.5 1.3 slice.135
  51.1 1.7 copy.33
  54.0 11.7 %cholesky.104 = f32[128,128]{1,0:T(8,128)S(1)} custom-call(f32[128,128]{1,0:T(8,128)S(1)} %cholesky.266), custom_call_target="Cholesky" | custom-call | tf_op jit(solution)/shard_map/jit(cholesky)/cholesky | solution.py:36
  65.7 9.8 %custom-call.31 = f32[1,128,128]{1,2,0:T(8,128)S(1)} custom-call(f32[1,128,128]{2,1,0:T(8,128)S(1)} %get-tuple-element.36), custom_call_target="InvertDiagBlocksLowerTriangular" | custom-call | tf_op jit(solution)/shard_map/jit(cholesky)/cholesky | solution.py:36
  75.7 1.2 constant_dynamic-update-slice_fusion.3
  76.9 1.3 convolution_subtract_fusion
  78.2 11.7 %cholesky.217 = f32[128,128]{1,0:T(8,128)S(1)} custom-call(f32[128,128]{1,0:T(8,128)S(1)} %cholesky.270), custom_call_target="Cholesky" | custom-call | tf_op jit(solution)/shard_map/jit(cholesky)/cholesky | solution.py:36
  89.9 9.9 %custom-call.32 = f32[1,128,128]{1,2,0:T(8,128)S(1)} custom-call(f32[1,128,128]{2,1,0:T(8,128)S(1)} %get-tuple-element.33), custom_call_target="InvertDiagBlocksLowerTriangular" | custom-call | tf_op jit(solution)/shard_map/jit(cholesky)/cholesky | solution.py:36
  100.1 1.3 convolution_subtract_fusion.1
  101.4 11.7 %cholesky.238 = f32[128,128]{1,0:T(8,128)S(1)} custom-call(f32[128,128]{1,0:T(8,128)S(1)} %cholesky.275), custom_call_target="Cholesky" | custom-call | tf_op jit(solution)/shard_map/jit(cholesky)/cholesky | solution.py:36
  113.9 9.8 %custom-call.33 = f32[1,128,128]{1,2,0:T(8,128)S(1)} custom-call(f32[1,128,128]{2,1,0:T(8,128)S(1)} %get-tuple-element.30), custom_call_target="InvertDiagBlocksLowerTriangular" | custom-call | tf_op jit(solution)/shard_map/jit(cholesky)/cholesky | solution.py:36
  123.9 1.2 convolution_subtract_fusion.5
  125.1 11.9 %cholesky.255 = f32[128,128]{1,0:T(8,128)S(1)} custom-call(f32[128,128]{1,0:T(8,128)S(1)} %convolution_subtract_fusion.5), custom_call_target="Cholesky" | custom-call | tf_op jit(solution)/shard_map/jit(cholesky)/cholesky | solution.py:36
  141.2 10.4 %while.1 = (s32[]{:T(128)}, f32[512,512]{1,0:T(8,128)S(1)}, s32[4,2]{0,1:T(2,128)S(1)}, f32[4,128,128]{2,1,0:T(8,128)}, s32[]{:T(128)}) while((s32[]{:T(128)}, f32[512,512]{1,0:T(8,128)S(1)}, s32[4,2]{0,1:T(2,128)S(1)}, f32[4,128,128]{2,1,0:T(8,128)}, s32[]{:T(128)}) %tuple.35), condition=%wide.while_cond, body=%wide.while_body.sunk | while | flops 2 | bytes 132705 | solution.py:37
  141.8 2.0 bitcast_dynamic-update-slice_fusion.2
  144.4 2.0 bitcast_dynamic-update-slice_fusion.2
  147.0 2.0 bitcast_dynamic-update-slice_fusion.2
  149.6 2.0 bitcast_dynamic-update-slice_fusion.2
  151.6 40.1 %custom-call.34 = f32[4,128,128]{1,2,0:T(8,128)S(1)} custom-call(f32[4,128,128]{2,1,0:T(8,128)} %get-tuple-element.9), custom_call_target="InvertDiagBlocksLowerTriangular" | custom-call | tf_op jit(solution)/shard_map/jit(_solve_triangular)/triangular_solve | solution.py:37
  194.5 2.6 %collective-permute-start.1 = (f32[1,128,128]{2,1,0:T(8,128)S(1)}, f32[1,128,128]{2,1,0:T(8,128)S(1)}, u32[]{:S(2)}, u32[]{:S(2)}) collective-permute-start(f32[1,128,128]{2,1,0:T(8,128)S(1)} %get-tuple-element.26), channel_id=1, source_target_pairs={{0,7},{1,0},{2,1},{3,2},{4,3},{5,4},{6,5},{7,6},{8,15},{9,8},{10,9... | collective-permute-start | bytes 196616 | tf_op jit(solution)/shard_map/ppermute | solution.py:12
  197.7 2.0 collective-permute-done
  199.7 1.6 collective-permute-done.2
  203.2 32.7 %all-reduce.3.cloned.1.call-done = f32[1,128,128]{2,1,0:T(8,128)} async-done(((f32[1,128,128]{2,1,0:T(8,128)}), f32[1,128,128]{2,1,0:T(8,128)}) %all-reduce.3.cloned.1.call-update) | async-done | bytes 65552 | tf_op jit(solution)/shard_map/psum | solution.py:86
  235.9 1.5 copy.66
  (87 shorter events, 20.0 us)
Async XLA Ops:
  9.8 10.6 %all-to-all-start = ((s32[8,1,8]{2,1,0:T(1,128)}), s32[8,1,8]{2,1,0:T(1,128)S(1)}, u32[]{:S(2)}, u32[]{:S(2)}) async-start(s32[8,1,8]{2,1,0:T(1,128)} %bitcast.6), calls=%async_computation | async-start | bytes 8192 | tf_op jit(solution)/shard_map/all_to_all | solution.py:69
  18.7 6.0 %copy-start.6 = (s32[1,8]{1,0:T(1,128)S(1)}, s32[1,8]{1,0:T(1,128)}, u32[]{:S(2)}) copy-start(s32[1,8]{1,0:T(1,128)} %param.13) | copy-start | bytes 100
  18.7 6.0 %copy-start.7 = (s32[1,8]{1,0:T(1,128)S(1)}, s32[1,8]{1,0:T(1,128)}, u32[]{:S(2)}) copy-start(s32[1,8]{1,0:T(1,128)} %param.12) | copy-start | bytes 100
  18.7 7.3 %copy-start.8 = (s32[50]{0:T(128)S(1)}, s32[50]{0:T(128)}, u32[]{:S(2)}) copy-start(s32[50]{0:T(128)} %constant.222) | copy-start | bytes 604
  18.7 7.3 %copy-start.4 = (f32[1,8,640]{2,1,0:T(8,128)S(1)}, f32[1,8,640]{2,1,0:T(8,128)}, u32[]{:S(2)}) copy-start(f32[1,8,640]{2,1,0:T(8,128)} %param.14) | copy-start | bytes 61444
  20.4 19.6 %all-to-all-start.1 = ((bf16[8,8,64,128]{3,1,2,0:T(8,128)(2,1)}), bf16[8,8,64,128]{3,1,2,0:T(8,128)(2,1)S(1)}, u32[]{:S(2)}, u32[]{:S(2)}) async-start(bf16[8,8,64,128]{3,1,2,0:T(8,128)(2,1)} %copy.28), calls=%async_computation.1 | async-start | bytes 2097152 | tf_op jit(solution)/shard_map/all_to_all | solution.py:62
  24.6 211.2 %all-reduce.3.cloned.1.call-start = ((), (), s32[]{:S(2)}) async-start(), calls=%async_computation.2 | async-start | bytes 131072 | tf_op jit(solution)/shard_map/psum | solution.py:86
  40.9 0.7 copy-start.5
  47.0 2.0 copy-start
  49.5 1.5 copy-start.1
  51.1 1.7 copy-start.2
  53.0 1.0 copy-start.3
  194.4 5.3 %collective-permute-start = (f32[1,128,128]{2,1,0:T(8,128)S(1)}, f32[1,128,128]{2,1,0:T(8,128)S(1)}, u32[]{:S(2)}, u32[]{:S(2)}) collective-permute-start(f32[1,128,128]{2,1,0:T(8,128)S(1)} %get-tuple-element.24), channel_id=1, source_target_pairs={{0,1},{1,2},{2,3},{3,4},{4,5},{5,6},{6,7},{7,0},{8,9},{9,10},{10,1... | collective-permute-start | bytes 196616 | tf_op jit(solution)/shard_map/ppermute | solution.py:12
  194.5 5.3 %collective-permute-start.1 = (f32[1,128,128]{2,1,0:T(8,128)S(1)}, f32[1,128,128]{2,1,0:T(8,128)S(1)}, u32[]{:S(2)}, u32[]{:S(2)}) collective-permute-start(f32[1,128,128]{2,1,0:T(8,128)S(1)} %get-tuple-element.26), channel_id=1, source_target_pairs={{0,7},{1,0},{2,1},{3,2},{4,3},{5,4},{6,5},{7,6},{8,15},{9,8},{10,9... | collective-permute-start | bytes 196616 | tf_op jit(solution)/shard_map/ppermute | solution.py:12
  197.1 4.3 %collective-permute-start.2 = (f32[1,128,128]{2,1,0:T(8,128)S(1)}, f32[1,128,128]{2,1,0:T(8,128)S(1)}, u32[]{:S(2)}, u32[]{:S(2)}) collective-permute-start(f32[1,128,128]{2,1,0:T(8,128)S(1)} %get-tuple-element.25), channel_id=1, source_target_pairs={{0,4},{1,5},{2,6},{3,7},{4,0},{5,1},{6,2},{7,3},{8,12},{9,13},{10,... | collective-permute-start | bytes 196616 | tf_op jit(solution)/shard_map/ppermute | solution.py:12
Sparse Core Ops, SparseCore 0:
  202.1 33.6 all-reduce.2
where the time goes:
time: 245 us; the launch traced here: 244 us
  other arithmetic  126 us (51%)
  waiting for transfers between devices  49 us (20%)
  local copies, waits for them, and re-layouts  30.5 us (12%)
  between operations  17.7 us (7%)
  starting transfers between devices  12.7 us (5%)
  matrix products  8.06 us (3%)
    another operation x14, other arithmetic, front_factor(): jnp.linalg.cholesky(front_matrix[:elimination_count, :elimination_count])  78.7 us
    another operation x3, other arithmetic, front_factor(): jax.scipy.linalg.solve_triangular(lower_triangle, front_matrix[eliminatio...  40.4 us
    psum x1, waiting for transfers between devices, body(): total = lax.psum(local_sum, 'grp')  32.7 us
    all_to_all x1, waiting for transfers between devices, body(): lax.all_to_all(outgoing.reshape(width, room, rows, column_indices), 'sep'...  12.6 us
    another operation x12, local copies, waits for them, and re-layouts  10.4 us
    another operation x6, matrix products, front_factor(): jnp.linalg.cholesky(front_matrix[:elimination_count, :elimination_count])  5.47 us
    all_to_all x1, starting transfers between devices, body(): lax.all_to_all(labels.reshape(width, room), 'sep', split_axis=0, concat_a...  5.2 us
  transfers between devices with their start and end apart: 6, of which 4 were waited for; matrix products, arithmetic and copies ran while one was open for 3% of the time, Pallas kernels for 0%

commit v1 on v0

--- a/solution.py
+++ b/solution.py
@@ -5,6 +5,15 @@
 from jax.sharding import PartitionSpec as P
 
 POS = 30
+
+
+def doubling_sum(x, axis):
+    size = lax.axis_size(axis)
+    summed, stride = (x, 1)
+    while stride < size:
+        summed = summed + lax.ppermute(summed, axis, [(i, i ^ stride) for i in range(size)])
+        stride = 2 * stride
+    return summed
 
 
 def passed_along(shard, axis, by):
@@ -83,7 +92,7 @@
     for offset in (1, -1, width // 2):
         piece = jnp.where(distance == offset % width, schur, 0.0)[None]
         local_sum = local_sum + passed_along(piece, "sep", offset)
-    total = lax.psum(local_sum, "grp")
+    total = doubling_sum(local_sum, "grp")
     return (factor[None, None], total)
 
 

time: 245 us -> 206 us (0.84)
  waiting for transfers between devices: 49 us -> 19.9 us
  between operations: 17.7 us -> 4.35 us
  starting transfers between devices: 12.7 us -> 17.4 us
    psum x1 -> x0, waiting for transfers between devices: 32.7 us -> none  [body(): total = lax.psum(local_sum, 'grp')]
    ppermute x0 -> x2, starting transfers between devices: none -> 4.8 us  [doubling_sum(): lax.ppermute(summed, axis, [(i, i ^ stride) for i in range(size)])]
    ppermute x0 -> x2, waiting for transfers between devices: none -> 3.77 us  [doubling_sum(): lax.ppermute(summed, axis, [(i, i ^ stride) for i in range(size)])]
  transfers between devices with their start and end apart: 6 -> 7, of which waited for: 4 -> 5; matrix products, arithmetic and copies ran while one was open for 3% -> 4% of each run, Pallas kernels for 0% -> 0%
where the time goes in v1:
time: 206 us
  other arithmetic  126 us (61%)
  local copies, waits for them, and re-layouts  29.5 us (14%)
  waiting for transfers between devices  19.9 us (10%)
  starting transfers between devices  17.4 us (8%)
  matrix products  8.07 us (4%)
  between operations  4.35 us (2%)
    another operation x14, other arithmetic, front_factor(): jnp.linalg.cholesky(front_matrix[:elimination_count, :elimination_count])  78.7 us
    another operation x3, other arithmetic, front_factor(): jax.scipy.linalg.solve_triangular(lower_triangle, front_matrix[eliminatio...  40.4 us
    all_to_all x1, waiting for transfers between devices, body(): lax.all_to_all(outgoing.reshape(width, room, rows, column_indices), 'sep'...  12.4 us
    another operation x12, local copies, waits for them, and re-layouts  10.9 us
    another operation x6, matrix products, front_factor(): jnp.linalg.cholesky(front_matrix[:elimination_count, :elimination_count])  5.47 us
    all_to_all x1, starting transfers between devices, body(): lax.all_to_all(labels.reshape(width, room), 'sep', split_axis=0, concat_a...  5.2 us
    ppermute x2, starting transfers between devices, doubling_sum(): lax.ppermute(summed, axis, [(i, i ^ stride) for i in range(size)])  4.8 us
    all_to_all x1, starting transfers between devices, body(): lax.all_to_all(outgoing.reshape(width, room, rows, column_indices), 'sep'...  4.2 us
  transfers between devices with their start and end apart: 7, of which 5 were waited for; matrix products, arithmetic and copies ran while one was open for 4% of the time, Pallas kernels for 0%

profile of v1, /device:TPU:0, one launch (start us, length us, event | category | flops | bytes accessed | tf_op | source)
XLA Modules:
  0.0 205.7 jit_solution(17288341231316802575)
XLA Ops:
  3.3 5.2 %all-to-all-start = ((s32[8,1,8]{2,1,0:T(1,128)}), s32[8,1,8]{2,1,0:T(1,128)S(1)}, u32[]{:S(2)}, u32[]{:S(2)}) async-start(s32[8,1,8]{2,1,0:T(1,128)} %bitcast.6), calls=%async_computation | async-start | bytes 8192 | tf_op jit(solution)/shard_map/all_to_all | solution.py:78
  8.7 3.4 %scatter_fusion = bf16[64,64,128]{2,1,0:T(8,128)(2,1)S(1)} fusion(bf16[64,64,128]{2,1,0:T(8,128)(2,1)S(1)} %broadcast_in_dim.90, s32[32]{0:T(128)S(1)} %fusion.44, bf16[32,64,128]{2,1,0:T(8,128)(2,1)} %bitcast.120), kind=kCustom, calls=%fused_computation.2 | custom fusion | bytes 1572992 | tf_op jit(solution)/shard_map/scatter | solution.py:68
  12.2 1.7 copy.28
  13.9 4.2 %all-to-all-start.1 = ((bf16[8,8,64,128]{3,1,2,0:T(8,128)(2,1)}), bf16[8,8,64,128]{3,1,2,0:T(8,128)(2,1)S(1)}, u32[]{:S(2)}, u32[]{:S(2)}) async-start(bf16[8,8,64,128]{3,1,2,0:T(8,128)(2,1)} %copy.28), calls=%async_computation.1 | async-start | bytes 2097152 | tf_op jit(solution)/shard_map/all_to_all | solution.py:71
  21.0 12.4 %all-to-all-done.1 = bf16[8,8,64,128]{3,1,2,0:T(8,128)(2,1)S(1)} async-done(((bf16[8,8,64,128]{3,1,2,0:T(8,128)(2,1)}), bf16[8,8,64,128]{3,1,2,0:T(8,128)(2,1)S(1)}, u32[]{:S(2)}, u32[]{:S(2)}) %all-to-all-start.1) | async-done | bytes 1048608 | tf_op jit(solution)/shard_map/all_to_all | solution.py:71
  36.2 1.6 copy.49
  37.8 2.7 %copy.32 = f32[640,640]{0,1:T(8,128)} copy(f32[640,640]{1,0:T(8,128)} %bitcast.118) | data formatting | bytes 3276800 | tf_op jit(solution)/shard_map/reshape | solution.py:42
  40.5 2.0 fusion.7
  43.0 1.2 slice.135
  44.6 1.7 copy.33
  47.4 11.7 %cholesky.104 = f32[128,128]{1,0:T(8,128)S(1)} custom-call(f32[128,128]{1,0:T(8,128)S(1)} %cholesky.266), custom_call_target="Cholesky" | custom-call | tf_op jit(solution)/shard_map/jit(cholesky)/cholesky | solution.py:45
  59.2 9.8 %custom-call.31 = f32[1,128,128]{1,2,0:T(8,128)S(1)} custom-call(f32[1,128,128]{2,1,0:T(8,128)S(1)} %get-tuple-element.36), custom_call_target="InvertDiagBlocksLowerTriangular" | custom-call | tf_op jit(solution)/shard_map/jit(cholesky)/cholesky | solution.py:45
  69.1 1.2 constant_dynamic-update-slice_fusion.3
  70.4 1.3 convolution_subtract_fusion
  71.6 11.7 %cholesky.217 = f32[128,128]{1,0:T(8,128)S(1)} custom-call(f32[128,128]{1,0:T(8,128)S(1)} %cholesky.270), custom_call_target="Cholesky" | custom-call | tf_op jit(solution)/shard_map/jit(cholesky)/cholesky | solution.py:45
  83.4 9.9 %custom-call.32 = f32[1,128,128]{1,2,0:T(8,128)S(1)} custom-call(f32[1,128,128]{2,1,0:T(8,128)S(1)} %get-tuple-element.33), custom_call_target="InvertDiagBlocksLowerTriangular" | custom-call | tf_op jit(solution)/shard_map/jit(cholesky)/cholesky | solution.py:45
  93.6 1.3 convolution_subtract_fusion.1
  94.9 11.7 %cholesky.238 = f32[128,128]{1,0:T(8,128)S(1)} custom-call(f32[128,128]{1,0:T(8,128)S(1)} %cholesky.275), custom_call_target="Cholesky" | custom-call | tf_op jit(solution)/shard_map/jit(cholesky)/cholesky | solution.py:45
  107.3 9.8 %custom-call.33 = f32[1,128,128]{1,2,0:T(8,128)S(1)} custom-call(f32[1,128,128]{2,1,0:T(8,128)S(1)} %get-tuple-element.30), custom_call_target="InvertDiagBlocksLowerTriangular" | custom-call | tf_op jit(solution)/shard_map/jit(cholesky)/cholesky | solution.py:45
  118.6 11.9 %cholesky.255 = f32[128,128]{1,0:T(8,128)S(1)} custom-call(f32[128,128]{1,0:T(8,128)S(1)} %convolution_subtract_fusion.5), custom_call_target="Cholesky" | custom-call | tf_op jit(solution)/shard_map/jit(cholesky)/cholesky | solution.py:45
  134.6 10.9 %while.1 = (s32[]{:T(128)}, f32[512,512]{1,0:T(8,128)S(1)}, s32[4,2]{0,1:T(2,128)S(1)}, f32[4,128,128]{2,1,0:T(8,128)}, s32[]{:T(128)}) while((s32[]{:T(128)}, f32[512,512]{1,0:T(8,128)S(1)}, s32[4,2]{0,1:T(2,128)S(1)}, f32[4,128,128]{2,1,0:T(8,128)}, s32[]{:T(128)}) %tuple.35), condition=%wide.while_cond, body=%wide.while_body.sunk | while | flops 2 | bytes 132705 | solution.py:46
  135.3 2.0 bitcast_dynamic-update-slice_fusion.2
  138.0 2.0 bitcast_dynamic-update-slice_fusion.2
  140.8 2.1 bitcast_dynamic-update-slice_fusion.2
  143.5 2.0 bitcast_dynamic-update-slice_fusion.2
  145.5 40.1 %custom-call.34 = f32[4,128,128]{1,2,0:T(8,128)S(1)} custom-call(f32[4,128,128]{2,1,0:T(8,128)} %get-tuple-element.9), custom_call_target="InvertDiagBlocksLowerTriangular" | custom-call | tf_op jit(solution)/shard_map/jit(_solve_triangular)/triangular_solve | solution.py:46
  188.4 2.6 %collective-permute-start.1 = (f32[1,128,128]{2,1,0:T(8,128)S(1)}, f32[1,128,128]{2,1,0:T(8,128)S(1)}, u32[]{:S(2)}, u32[]{:S(2)}) collective-permute-start(f32[1,128,128]{2,1,0:T(8,128)S(1)} %get-tuple-element.26), channel_id=1, source_target_pairs={{0,7},{1,0},{2,1},{3,2},{4,3},{5,4},{6,5},{7,6},{8,15},{9,8},{10,9... | collective-permute-start | bytes 196616 | tf_op jit(solution)/shard_map/ppermute | solution.py:21
  191.6 2.1 %collective-permute-done = f32[1,128,128]{2,1,0:T(8,128)S(1)} collective-permute-done((f32[1,128,128]{2,1,0:T(8,128)S(1)}, f32[1,128,128]{2,1,0:T(8,128)S(1)}, u32[]{:S(2)}, u32[]{:S(2)}) %collective-permute-start) | collective-permute-done | bytes 65568 | tf_op jit(solution)/shard_map/ppermute | solution.py:21
  193.7 1.6 collective-permute-done.2
  195.3 1.6 collective-permute-start.3
  197.0 2.7 %collective-permute-done.3 = f32[1,128,128]{2,1,0:T(8,128)S(1)} collective-permute-done((f32[1,128,128]{2,1,0:T(8,128)S(1)}, f32[1,128,128]{2,1,0:T(8,128)S(1)}, u32[]{:S(2)}, u32[]{:S(2)}) %collective-permute-start.3) | collective-permute-done | bytes 65568 | tf_op jit(solution)/shard_map/ppermute | solution.py:14
  199.7 3.2 %collective-permute-start.4 = (f32[1,128,128]{2,1,0:T(8,128)S(1)}, f32[1,128,128]{2,1,0:T(8,128)S(1)}, u32[]{:S(2)}, u32[]{:S(2)}) collective-permute-start(f32[1,128,128]{2,1,0:T(8,128)S(1)} %add.113), channel_id=1, source_target_pairs={{0,16},{8,24},{16,0},{24,8},{1,17},{9,25},{17,1},{25,9},{2,18},{10... | collective-permute-start | bytes 196616 | tf_op jit(solution)/shard_map/ppermute | solution.py:14
  (89 shorter events, 22.8 us)
Async XLA Ops:
  3.3 10.6 %all-to-all-start = ((s32[8,1,8]{2,1,0:T(1,128)}), s32[8,1,8]{2,1,0:T(1,128)S(1)}, u32[]{:S(2)}, u32[]{:S(2)}) async-start(s32[8,1,8]{2,1,0:T(1,128)} %bitcast.6), calls=%async_computation | async-start | bytes 8192 | tf_op jit(solution)/shard_map/all_to_all | solution.py:78
  12.1 6.0 %copy-start.6 = (s32[1,8]{1,0:T(1,128)S(1)}, s32[1,8]{1,0:T(1,128)}, u32[]{:S(2)}) copy-start(s32[1,8]{1,0:T(1,128)} %param.13) | copy-start | bytes 100
  12.1 5.9 %copy-start.7 = (s32[1,8]{1,0:T(1,128)S(1)}, s32[1,8]{1,0:T(1,128)}, u32[]{:S(2)}) copy-start(s32[1,8]{1,0:T(1,128)} %param.12) | copy-start | bytes 100
  12.1 7.4 %copy-start.8 = (s32[50]{0:T(128)S(1)}, s32[50]{0:T(128)}, u32[]{:S(2)}) copy-start(s32[50]{0:T(128)} %constant.222) | copy-start | bytes 604
  12.2 7.4 %copy-start.4 = (f32[1,8,640]{2,1,0:T(8,128)S(1)}, f32[1,8,640]{2,1,0:T(8,128)}, u32[]{:S(2)}) copy-start(f32[1,8,640]{2,1,0:T(8,128)} %param.14) | copy-start | bytes 61444
  13.9 19.6 %all-to-all-start.1 = ((bf16[8,8,64,128]{3,1,2,0:T(8,128)(2,1)}), bf16[8,8,64,128]{3,1,2,0:T(8,128)(2,1)S(1)}, u32[]{:S(2)}, u32[]{:S(2)}) async-start(bf16[8,8,64,128]{3,1,2,0:T(8,128)(2,1)} %copy.28), calls=%async_computation.1 | async-start | bytes 2097152 | tf_op jit(solution)/shard_map/all_to_all | solution.py:71
  34.3 0.7 copy-start.5
  40.5 2.0 copy-start
  43.0 1.5 copy-start.1
  44.5 1.7 copy-start.2
  46.4 1.0 copy-start.3
  188.3 5.3 %collective-permute-start = (f32[1,128,128]{2,1,0:T(8,128)S(1)}, f32[1,128,128]{2,1,0:T(8,128)S(1)}, u32[]{:S(2)}, u32[]{:S(2)}) collective-permute-start(f32[1,128,128]{2,1,0:T(8,128)S(1)} %get-tuple-element.24), channel_id=1, source_target_pairs={{0,1},{1,2},{2,3},{3,4},{4,5},{5,6},{6,7},{7,0},{8,9},{9,10},{10,1... | collective-permute-start | bytes 196616 | tf_op jit(solution)/shard_map/ppermute | solution.py:21
  188.4 5.3 %collective-permute-start.1 = (f32[1,128,128]{2,1,0:T(8,128)S(1)}, f32[1,128,128]{2,1,0:T(8,128)S(1)}, u32[]{:S(2)}, u32[]{:S(2)}) collective-permute-start(f32[1,128,128]{2,1,0:T(8,128)S(1)} %get-tuple-element.26), channel_id=1, source_target_pairs={{0,7},{1,0},{2,1},{3,2},{4,3},{5,4},{6,5},{7,6},{8,15},{9,8},{10,9... | collective-permute-start | bytes 196616 | tf_op jit(solution)/shard_map/ppermute | solution.py:21
  191.0 4.3 %collective-permute-start.2 = (f32[1,128,128]{2,1,0:T(8,128)S(1)}, f32[1,128,128]{2,1,0:T(8,128)S(1)}, u32[]{:S(2)}, u32[]{:S(2)}) collective-permute-start(f32[1,128,128]{2,1,0:T(8,128)S(1)} %get-tuple-element.25), channel_id=1, source_target_pairs={{0,4},{1,5},{2,6},{3,7},{4,0},{5,1},{6,2},{7,3},{8,12},{9,13},{10,... | collective-permute-start | bytes 196616 | tf_op jit(solution)/shard_map/ppermute | solution.py:21
  195.3 4.3 %collective-permute-start.3 = (f32[1,128,128]{2,1,0:T(8,128)S(1)}, f32[1,128,128]{2,1,0:T(8,128)S(1)}, u32[]{:S(2)}, u32[]{:S(2)}) collective-permute-start(f32[1,128,128]{2,1,0:T(8,128)S(1)} %fusion.35), channel_id=1, source_target_pairs={{0,8},{8,0},{16,24},{24,16},{1,9},{9,1},{17,25},{25,17},{2,10},{10... | collective-permute-start | bytes 196616 | tf_op jit(solution)/shard_map/ppermute | solution.py:14
  199.7 5.4 %collective-permute-start.4 = (f32[1,128,128]{2,1,0:T(8,128)S(1)}, f32[1,128,128]{2,1,0:T(8,128)S(1)}, u32[]{:S(2)}, u32[]{:S(2)}) collective-permute-start(f32[1,128,128]{2,1,0:T(8,128)S(1)} %add.113), channel_id=1, source_target_pairs={{0,16},{8,24},{16,0},{24,8},{1,17},{9,25},{17,1},{25,9},{2,18},{10... | collective-permute-start | bytes 196616 | tf_op jit(solution)/shard_map/ppermute | solution.py:14
